TPU v7x, 32 devices: a whole 2x2x4 slice. The times are simulated.
32 devices in a mesh: seq: 4 (over z), head: 8 (over y, x, core).
Axes of the slice: x: 2, y: 2, z: 4, core: 2. Of those that a mesh axis runs over, the one named last changes fastest.
Arguments:
- inputs: bfloat16 [2048, 8192], P('seq'), may hold values from -6 to 6
- w_qkv: bfloat16 [3, 8192, 2048], P(None, None, 'head'), may hold values from -0.0625 to 0.0625
- w_out: bfloat16 [2048, 8192], P('head'), may hold values from -0.1875 to 0.1875
- turn_ids: int32 [4, 512], P('seq'), may hold values from 0 to 15, never falling along the last dimension, each value on 1 to 64 neighbouring positions
- picked: int32 [4, 64], P('seq'), may hold values from 0 to 511
- owners: int32 [256, 1], P('seq'), may hold values from 0 to 7; in each aligned block of 64 rows (0 to 63, 64 to 127, ...) at most 32 rows name the same one
- candidates: bfloat16 [2048, 8192], P(('seq', 'head')), may hold values from -0.25 to 0.25
Outputs:
- mixed: bfloat16 [2048, 8192], P('seq', 'head')
- scores: float32 [1024, 64], P(('seq', 'head'))
Inputs may be any that keep to these rules, and one draw needn't show every extreme that they name: `turn_ids`: within each session turn numbers start at 0, never fall, and each turn has 1 to 64 tokens. `owners`: among the 64 picked rows of one session no owner is named more than 32 times.
All inputs are finite; a program needn't handle non-finite values.
Results may differ from a plain program's by a relative error of at most 0.008.
Values may be sent and summed in bfloat16 or wider, within the bound.
No kernel may reach another device: no remote copies, remote signals or barrier semaphores. Data moves between devices by JAX's collectives and lax.ppermute only.
A program may use at most 128 MiB of HBM per device.

v0:
```python
import jax
import jax.numpy as jnp
from jax import lax
from jax.sharding import PartitionSpec as P

HDIM = 128


def carried_in(value, axis, join, neutral):
    count, mine = (lax.axis_size(axis), lax.axis_index(axis))
    pieces = lax.all_gather(value, axis)
    so_far = jnp.full_like(value, 0) + jnp.asarray(neutral, value.dtype)

    def lap(position, so_far):
        longer = join(so_far, pieces[position])
        return jnp.where(position < mine, longer, so_far)

    return lax.fori_loop(0, count - 1, lap, so_far)


def per_device(inputs, w_qkv, w_out, turn_ids, picked, owners, candidates):
    tokens_here = inputs.shape[0]
    model_width = inputs.shape[1]
    heads_here = w_qkv.shape[2] // HDIM
    n_head = lax.axis_size("head")
    col_count = model_width // n_head
    projected = lax.dot_general(
        inputs, w_qkv, (((1,), (1,)), ((), ())), preferred_element_type=jnp.float32
    ).astype(jnp.bfloat16)
    query = projected[:, 0].reshape(tokens_here, heads_here, HDIM)
    keys = projected[:, 1].reshape(tokens_here, heads_here, HDIM)
    values = projected[:, 2].reshape(tokens_here, heads_here, HDIM)
    states = jnp.einsum("thi,thj->hij", keys, values, preferred_element_type=jnp.float32)
    prefix = carried_in(states, "seq", jnp.add, jnp.zeros_like(states))
    prefix = prefix.astype(jnp.bfloat16)
    scores_local = jnp.einsum("thi,shi->hts", query, keys, preferred_element_type=jnp.float32)
    tok_pos = jnp.arange(tokens_here, dtype=jnp.int32)
    causal = tok_pos[:, None] >= tok_pos[None, :]
    weights = jnp.where(causal[None, :, :], scores_local, 0.0).astype(jnp.bfloat16)
    local_part = jnp.einsum("hts,shj->thj", weights, values, preferred_element_type=jnp.float32)
    carried = jnp.einsum("thi,hij->thj", query, prefix, preferred_element_type=jnp.float32)
    summed = local_part + carried
    normed = summed * lax.rsqrt(jnp.mean(summed * summed, axis=-1, keepdims=True) + 1e-05)
    attended = normed.astype(jnp.bfloat16).reshape(tokens_here, heads_here * HDIM)
    input_cols = lax.dynamic_slice_in_dim(inputs, lax.axis_index("head") * col_count, col_count, 1)
    w_cols = lax.all_to_all(w_out, "head", split_axis=1, concat_axis=0, tiled=True)
    branch = jnp.dot(
        lax.all_gather(attended, "head", axis=1, tiled=True),
        w_cols,
        preferred_element_type=jnp.float32,
    )
    mixed = (input_cols.astype(jnp.float32) + branch).astype(jnp.bfloat16)
    turn_row = turn_ids[0]
    pick_row = picked[0]
    r_dev = pick_row.shape[0]
    cap_rows = 4 * r_dev // n_head
    pick_hot = tok_pos[None, :] == pick_row[:, None]
    sel_turn = jnp.sum(jnp.where(pick_hot, turn_row[None, :], 0), axis=1)
    member = (turn_row[None, :] == sel_turn[:, None]) & (tok_pos[None, :] <= pick_row[:, None])
    row_count = jnp.sum(member.astype(jnp.float32), axis=1)
    pooled = jnp.dot(member.astype(jnp.bfloat16), mixed, preferred_element_type=jnp.float32)
    summary = (pooled / row_count[:, None]).astype(jnp.bfloat16)
    owner_row = owners[:, 0]
    row_pos = jnp.arange(r_dev, dtype=jnp.int32)
    head_pos = jnp.arange(n_head, dtype=jnp.int32)
    own_hot = (owner_row[:, None] == head_pos[None, :]).astype(jnp.int32)
    before = (row_pos[:, None] > row_pos[None, :]).astype(jnp.int32)
    slot_rank = jnp.sum(jnp.dot(before, own_hot) * own_hot, axis=1)
    slot_index = owner_row * cap_rows + slot_rank
    dispatch = (
        slot_index[None, :] == jnp.arange(n_head * cap_rows, dtype=jnp.int32)[:, None]
    ).astype(jnp.bfloat16)
    outgoing = jnp.dot(dispatch, summary, preferred_element_type=jnp.float32).astype(jnp.bfloat16)
    outgoing = outgoing.reshape(n_head, cap_rows, col_count)
    cand_parts = candidates.reshape(candidates.shape[0], n_head, col_count)
    scores = jnp.einsum(
        "skc,nsc->kn",
        lax.all_to_all(outgoing, "head", split_axis=0, concat_axis=0, tiled=True),
        cand_parts,
        preferred_element_type=jnp.float32,
    )
    return (mixed, scores)


def solution(mesh):
    return jax.shard_map(
        per_device,
        mesh=mesh,
        in_specs=(
            P("seq", None),
            P(None, None, "head"),
            P("head", None),
            P("seq", None),
            P("seq", None),
            P("seq", None),
            P(("seq", "head"), None),
        ),
        out_specs=(P("seq", "head"), P(("seq", "head"), None)),
        check_vma=False,
    )
```

profile of v0, /device:TPU:0, one launch (start us, length us, event | category | flops | bytes accessed | tf_op | source)
XLA Modules:
  0.0 109.3 jit_solution(5474585538032914516)
XLA Ops:
  7.2 6.4 %copy.43 = bf16[256,8192]{0,1:T(8,128)(2,1)} copy(bf16[256,8192]{1,0:T(8,128)(2,1)} %param.11) | data formatting | bytes 8388608 | tf_op args[2]
  13.6 5.2 %all-to-all-start = ((bf16[256,8,1024]{0,2,1:T(8,128)(2,1)}), bf16[256,8,1024]{0,2,1:T(8,128)(2,1)}, u32[]{:S(2)}, u32[]{:S(2)}) async-start(bf16[256,8,1024]{0,2,1:T(8,128)(2,1)} %bitcast.41), calls=%async_computation | async-start | bytes 8388608 | tf_op jit(solution)/shard_map/all_to_all | solution.py:46
  18.8 0.0 all-gather.3.cloned.1.call-start
  18.8 0.1 iota_compare_fusion
  18.9 12.2 %fusion.2 = bf16[512,3,256]{0,2,1:T(8,128)(2,1)S(1)} fusion(bf16[3,8192,256]{2,1,0:T(8,128)(2,1)} %param.10, bf16[512,8192]{1,0:T(8,128)(2,1)} %param.9), kind=kOutput, calls=%fused_computation.5 | convolution fusion | flops 6442844160 | bytes 21757952 | tf_op jit(solution)/shard_map/dot_general | solution.py:27
  31.1 0.1 fusion.29
  31.1 0.0 copy-start.3
  31.1 0.0 copy-start
  31.2 0.0 copy-start.1
  31.2 0.2 fusion.30
  31.4 17.1 %all-gather = f32[8,128,128]{2,1,0:T(8,128)S(1)} all-gather(f32[2,128,128]{2,1,0:T(8,128)S(1)} %fusion.30), channel_id=2, replica_groups=mesh['seq'=4,'head'=8] {'seq'}, dimensions={0}, use_global_device_ids=true | all-gather | bytes 655360 | tf_op jit(solution)/shard_map/all_gather | solution.py:11
  48.5 0.2 while.14
  48.7 0.3 fusion.23
  49.0 0.8 multiply_reduce_fusion
  49.8 0.7 multiply_convert_fusion
  50.5 0.0 all-gather.3.cloned.1.call-update
  50.6 0.0 copy-done.3
  50.6 0.1 fusion.9
  50.7 0.0 copy-done
  50.7 0.0 copy-done.1
  50.7 0.2 select_reduce_fusion
  50.9 0.2 convert_reduce_fusion
  51.1 19.6 %all-to-all-done = bf16[256,8,1024]{0,2,1:T(8,128)(2,1)} async-done(((bf16[256,8,1024]{0,2,1:T(8,128)(2,1)}), bf16[256,8,1024]{0,2,1:T(8,128)(2,1)}, u32[]{:S(2)}, u32[]{:S(2)}) %all-to-all-start) | async-done | bytes 4194336 | tf_op jit(solution)/shard_map/all_to_all | solution.py:46
  70.8 6.5 %copy.44 = bf16[8,256,1024]{2,1,0:T(8,128)(2,1)} copy(bf16[8,256,1024]{1,2,0:T(8,128)(2,1)} %bitcast.8) | data formatting | bytes 8388608 | tf_op jit(solution)/shard_map/all_to_all | solution.py:46
  77.2 5.9 %all-gather.3.cloned.1.call-done = bf16[512,2048]{0,1:T(8,128)(2,1)} async-done(((bf16[512,256]{0,1:T(8,128)(2,1)}), bf16[512,2048]{0,1:T(8,128)(2,1)}) %all-gather.3.cloned.1.call-update) | async-done | bytes 2097168 | tf_op jit(solution)/shard_map/all_gather | solution.py:48
  83.1 0.0 copy-start.2
  83.1 5.5 %add_convert_fusion = bf16[512,1024]{1,0:T(8,128)(2,1)S(1)} fusion(bf16[512,2048]{0,1:T(8,128)(2,1)} %all-gather.3.cloned.1.call-done, bf16[2048,1024]{1,0:T(8,128)(2,1)} %bitcast.42, bf16[512,8192]{1,0:T(8,128)(2,1)} %param.9, s32[]{:T(128)S(6)} %select_n.32), kind=kOutput, calls=%fused_computation.3 | convolution fusion | flops 2149056512 | bytes 8388612 | tf_op jit(solution)/shard_map/dot_general | solution.py:47
  88.6 0.0 copy-start.4
  88.6 0.5 convolution_convert_fusion
  89.2 12.3 %all_to_all.24 = bf16[8,32,1024]{2,1,0:T(8,128)(2,1)S(1)} all-to-all(bf16[8,32,1024]{2,1,0:T(8,128)(2,1)S(1)} %bitcast.51), channel_id=1, replica_groups=mesh['seq'=4,'head'=8] {'head'}, dimensions={0} | all-to-all | bytes 1048576 | tf_op jit(solution)/shard_map/all_to_all | solution.py:78
  101.4 0.0 copy-done.2
  101.4 1.0 convolution_bitcast_fusion
  102.5 0.0 copy-done.4
  (6 shorter events, 0.1 us)
Async XLA Ops:
  13.6 57.2 %all-to-all-start = ((bf16[256,8,1024]{0,2,1:T(8,128)(2,1)}), bf16[256,8,1024]{0,2,1:T(8,128)(2,1)}, u32[]{:S(2)}, u32[]{:S(2)}) async-start(bf16[256,8,1024]{0,2,1:T(8,128)(2,1)} %bitcast.41), calls=%async_computation | async-start | bytes 8388608 | tf_op jit(solution)/shard_map/all_to_all | solution.py:46
  18.8 64.3 %all-gather.3.cloned.1.call-start = ((), (), s32[]{:S(2)}) async-start(), calls=%async_computation.2 | async-start | bytes 2359296 | tf_op jit(solution)/shard_map/all_gather | solution.py:48
  31.1 19.4 %copy-start.3 = (s32[64,1]{0,1:T(1,128)S(1)}, s32[64,1]{0,1:T(1,128)}, u32[]{:S(2)}) copy-start(s32[64,1]{0,1:T(1,128)} %param.14) | copy-start | bytes 772
  31.1 19.6 %copy-start = (s32[1,512]{1,0:T(1,128)S(1)}, s32[1,512]{1,0:T(1,128)}, u32[]{:S(2)}) copy-start(s32[1,512]{1,0:T(1,128)} %param.12) | copy-start | bytes 6148
  31.2 19.6 %copy-start.1 = (s32[1,64]{1,0:T(1,128)S(1)}, s32[1,64]{1,0:T(1,128)}, u32[]{:S(2)}) copy-start(s32[1,64]{1,0:T(1,128)} %param.13) | copy-start | bytes 772
  83.1 18.3 %copy-start.2 = (bf16[64,8192]{1,0:T(8,128)(2,1)S(1)}, bf16[64,8192]{1,0:T(8,128)(2,1)}, u32[]{:S(2)}) copy-start(bf16[64,8192]{1,0:T(8,128)(2,1)} %param.15) | copy-start | bytes 3145732
  88.6 13.8 %copy-start.4 = (bf16[512,1024]{1,0:T(8,128)(2,1)}, bf16[512,1024]{1,0:T(8,128)(2,1)S(1)}, u32[]{:S(2)}) copy-start(bf16[512,1024]{1,0:T(8,128)(2,1)S(1)} %add_convert_fusion) | copy-start | bytes 3145732
Sparse Core Ops, SparseCore 0:
  50.7 32.3 all-gather.2
where the time goes:
time: 110 us; the launch traced here: 109 us
  blocking collectives  29.4 us (27%)
  waiting for transfers between devices  25.5 us (23%)
  matrix products  20.7 us (19%)
  between operations  14.2 us (13%)
  local copies, waits for them, and re-layouts  13 us (12%)
  starting transfers between devices  5.23 us (5%)
  other arithmetic  1.34 us (1%)
    all_to_all x1, waiting for transfers between devices, per_device(): lax.all_to_all(w_out, 'head', split_axis=1, concat_axis=0, tiled=True)  19.6 us
    all_gather x1, blocking collectives, carried_in(): pieces = lax.all_gather(value, axis)  17.1 us
    all_to_all x1, blocking collectives, per_device(): lax.all_to_all(outgoing, 'head', split_axis=0, concat_axis=0, tiled=True)  12.3 us
    dot_general x1, matrix products, per_device(): lax.dot_general(inputs, w_qkv, (((1,), (1,)), ((), ())), preferred_elemen...  12.2 us
    all_to_all x1, local copies, waits for them, and re-layouts, per_device(): lax.all_to_all(w_out, 'head', split_axis=1, concat_axis=0, tiled=True)  6.48 us
    unnamed x11, local copies, waits for them, and re-layouts  6.43 us
    all_gather x1, waiting for transfers between devices, per_device(): lax.all_gather(attended, 'head', axis=1, tiled=True)  5.86 us
    dot_general x1, matrix products, per_device(): jnp.dot(lax.all_gather(attended, 'head', axis=1, tiled=True), w_cols, pre...  5.52 us
  transfers between devices with their start and end apart: 2, of which 2 were waited for; matrix products, arithmetic and copies ran while one was open for 20% of the time, Pallas kernels for 0%

commit v1 on v0

--- a/solution.py
+++ b/solution.py
@@ -45,7 +45,9 @@
     input_cols = lax.dynamic_slice_in_dim(inputs, lax.axis_index("head") * col_count, col_count, 1)
     w_cols = lax.all_to_all(w_out, "head", split_axis=1, concat_axis=0, tiled=True)
     branch = jnp.dot(
-        lax.all_gather(attended, "head", axis=1, tiled=True),
+        jnp.concatenate(
+            lax.all_to_all(jnp.stack([attended] * lax.axis_size("head")), "head", 0, 0), axis=1
+        ),
         w_cols,
         preferred_element_type=jnp.float32,
     )

time: 110 us -> 139 us (1.26)
  waiting for transfers between devices: 25.5 us -> 62.3 us
  between operations: 14.2 us -> 0.79 us
  starting transfers between devices: 5.23 us -> 8.27 us
  matrix products: 20.7 us -> 22.3 us
  local copies, waits for them, and re-layouts: 13 us -> 14.6 us
    all_to_all x1, waiting for transfers between devices: 19.6 us -> 48.5 us  [per_device(): lax.all_to_all(w_out, 'head', split_axis=1, concat_axis=0, tiled=True)]
    all_to_all x0 -> x1, waiting for transfers between devices: none -> 13.8 us  [per_device(): lax.all_to_all(jnp.stack([attended] * lax.axis_size('head')), 'head', 0, 0)]
    all_gather x1 -> x0, waiting for transfers between devices: 5.86 us -> none  [per_device(): lax.all_gather(attended, 'head', axis=1, tiled=True)]
    all_to_all x0 -> x1, starting transfers between devices: none -> 3.72 us  [per_device(): lax.all_to_all(jnp.stack([attended] * lax.axis_size('head')), 'head', 0, 0)]
    another operation x0 -> x2, local copies, waits for them, and re-layouts: none -> 1.66 us  [per_device(): jnp.stack([attended] * lax.axis_size('head'))]
    unnamed x11 -> x9, local copies, waits for them, and re-layouts: 6.43 us -> 6.4 us
  transfers between devices with their start and end apart: 2 -> 2, of which waited for: 2 -> 2; matrix products, arithmetic and copies ran while one was open for 20% -> 10% of each run, Pallas kernels for 0% -> 0%
where the time goes in v1:
time: 139 us; the launch traced here: 138 us
  waiting for transfers between devices  62.3 us (45%)
  blocking collectives  29.5 us (21%)
  matrix products  22.3 us (16%)
  local copies, waits for them, and re-layouts  14.6 us (11%)
  starting transfers between devices  8.27 us (6%)
    all_to_all x1, waiting for transfers between devices, per_device(): lax.all_to_all(w_out, 'head', split_axis=1, concat_axis=0, tiled=True)  48.5 us
    all_gather x1, blocking collectives, carried_in(): pieces = lax.all_gather(value, axis)  17.4 us
    all_to_all x1, waiting for transfers between devices, per_device(): lax.all_to_all(jnp.stack([attended] * lax.axis_size('head')), 'head', 0, 0)  13.8 us
    dot_general x1, matrix products, per_device(): lax.dot_general(inputs, w_qkv, (((1,), (1,)), ((), ())), preferred_elemen...  12.3 us
    all_to_all x1, blocking collectives, per_device(): lax.all_to_all(outgoing, 'head', split_axis=0, concat_axis=0, tiled=True)  12.1 us
    all_to_all x1, local copies, waits for them, and re-layouts, per_device(): lax.all_to_all(w_out, 'head', split_axis=1, concat_axis=0, tiled=True)  6.44 us
    unnamed x9, local copies, waits for them, and re-layouts  6.4 us
    dot_general x1, matrix products, per_device(): jnp.dot(jnp.concatenate(lax.all_to_all(jnp.stack([attended] * lax.axis_si...  5.79 us
  transfers between devices with their start and end apart: 2, of which 2 were waited for; matrix products, arithmetic and copies ran while one was open for 10% of the time, Pallas kernels for 0%

profile of v1, /device:TPU:0, one launch (start us, length us, event | category | flops | bytes accessed | tf_op | source)
XLA Modules:
  0.0 138.4 jit_solution(213632650046916514)
XLA Ops:
  0.6 0.1 iota_compare_fusion
  0.7 12.3 %fusion.6 = bf16[512,3,256]{0,2,1:T(8,128)(2,1)S(1)} fusion(bf16[3,8192,256]{2,1,0:T(8,128)(2,1)} %param.10, bf16[512,8192]{1,0:T(8,128)(2,1)} %param.9), kind=kOutput, calls=%fused_computation.9 | convolution fusion | flops 6442844160 | bytes 21757952 | tf_op jit(solution)/shard_map/dot_general | solution.py:27
  13.0 0.1 fusion.37
  13.1 0.2 fusion.38
  13.3 17.4 %all-gather = f32[8,128,128]{2,1,0:T(8,128)S(1)} all-gather(f32[2,128,128]{2,1,0:T(8,128)S(1)} %fusion.38), channel_id=2, replica_groups=mesh['seq'=4,'head'=8] {'seq'}, dimensions={0}, use_global_device_ids=true | all-gather | bytes 655360 | tf_op jit(solution)/shard_map/all_gather | solution.py:11
  30.7 0.2 while.14
  30.9 0.3 fusion.31
  31.1 0.8 multiply_reduce_fusion
  32.0 0.1 copy.39
  32.2 1.5 %stack.3 = bf16[8,512,256]{2,1,0:T(8,128)(2,1)} broadcast(bf16[512,256]{1,0:T(8,128)(2,1)S(1)} %copy.39), dimensions={1,2} | broadcast | bytes 2359296 | tf_op jit(solution)/shard_map/stack | solution.py:49
  33.7 3.7 %all-to-all-start = ((bf16[8,512,256]{2,1,0:T(8,128)(2,1)}), bf16[8,512,256]{2,1,0:T(8,128)(2,1)S(1)}, u32[]{:S(2)}, u32[]{:S(2)}) async-start(bf16[8,512,256]{2,1,0:T(8,128)(2,1)} %stack.3), calls=%async_computation | async-start | bytes 4194304 | tf_op jit(solution)/shard_map/all_to_all | solution.py:49
  37.4 6.4 %copy.40 = bf16[256,8192]{0,1:T(8,128)(2,1)} copy(bf16[256,8192]{1,0:T(8,128)(2,1)} %param.11) | data formatting | bytes 8388608 | tf_op args[2]
  43.8 6.4 %copy.41 = bf16[256,8,1024]{2,0,1:T(8,128)(2,1)} copy(bf16[256,8,1024]{0,2,1:T(8,128)(2,1)} %bitcast.51) | data formatting | bytes 8388608 | tf_op jit(solution)/shard_map/all_to_all | solution.py:46
  50.2 0.0 copy-start.3
  50.2 0.0 copy-start
  50.2 0.0 copy-start.1
  50.2 13.8 %all-to-all-done = bf16[8,512,256]{2,1,0:T(8,128)(2,1)S(1)} async-done(((bf16[8,512,256]{2,1,0:T(8,128)(2,1)}), bf16[8,512,256]{2,1,0:T(8,128)(2,1)S(1)}, u32[]{:S(2)}, u32[]{:S(2)}) %all-to-all-start) | async-done | bytes 2097184 | tf_op jit(solution)/shard_map/all_to_all | solution.py:49
  64.0 4.5 %all-to-all-start.1 = ((bf16[256,8,1024]{2,0,1:T(8,128)(2,1)}), bf16[256,8,1024]{2,0,1:T(8,128)(2,1)}, u32[]{:S(2)}, u32[]{:S(2)}) async-start(bf16[256,8,1024]{2,0,1:T(8,128)(2,1)} %copy.41), calls=%async_computation.1 | async-start | bytes 8388608 | tf_op jit(solution)/shard_map/all_to_all | solution.py:46
  68.6 0.0 copy-done.3
  68.6 0.1 fusion.17
  68.7 0.0 copy-done
  68.7 0.0 copy-done.1
  68.8 0.2 select_reduce_fusion
  68.9 0.2 convert_reduce_fusion
  69.1 0.0 copy-start.2
  69.2 48.5 %all-to-all-done.1 = bf16[256,8,1024]{2,0,1:T(8,128)(2,1)} async-done(((bf16[256,8,1024]{2,0,1:T(8,128)(2,1)}), bf16[256,8,1024]{2,0,1:T(8,128)(2,1)}, u32[]{:S(2)}, u32[]{:S(2)}) %all-to-all-start.1) | async-done | bytes 4194336 | tf_op jit(solution)/shard_map/all_to_all | solution.py:46
  117.7 5.8 %fusion.4 = bf16[512,1024]{1,0:T(8,128)(2,1)} fusion(bf16[256,8,1024]{2,0,1:T(8,128)(2,1)} %all-to-all-done.1, bf16[8,512,256]{2,1,0:T(8,128)(2,1)S(1)} %all-to-all-done, bf16[512,8192]{1,0:T(8,128)(2,1)} %param.9, s32[]{:T(128)S(6)} %select_n.32), kind=kOutput, calls=%fused_computation.6 | convolution fusion | flops 2149056512 | bytes 8388612 | tf_op jit(solution)/shard_map/dot_general | solution.py:47
  123.5 1.8 %convolution_convert_fusion = bf16[256,1024]{1,0:T(8,128)(2,1)S(1)} fusion(bf16[512,1024]{1,0:T(8,128)(2,1)} %fusion.4, f32[64]{0:T(128)S(1)} %convert_reduce_fusion, s32[64]{0:T(128)S(1)} %bitcast.66, s32[512]{0:T(512)S(1)} %bitcast.63, s32[64]{0:T(128)S(1)} %multiply_add_fusion, s32[64]{0:T(128)S(1)} %select_reduce_fusion), kind=kOutput, calls=%fused_computation.11 | convolution fusion | flops 101171200 | bytes 1575936 | tf_op jit(solution)/shard_map/dot_general | solution.py:75
  125.2 12.1 %all_to_all.26 = bf16[8,32,1024]{2,1,0:T(8,128)(2,1)S(1)} all-to-all(bf16[8,32,1024]{2,1,0:T(8,128)(2,1)S(1)} %bitcast.60), channel_id=1, replica_groups=mesh['seq'=4,'head'=8] {'head'}, dimensions={0} | all-to-all | bytes 1048576 | tf_op jit(solution)/shard_map/all_to_all | solution.py:80
  137.4 0.0 copy-done.2
  137.4 1.0 convolution_bitcast_fusion
  (7 shorter events, 0.2 us)
Async XLA Ops:
  33.7 30.3 %all-to-all-start = ((bf16[8,512,256]{2,1,0:T(8,128)(2,1)}), bf16[8,512,256]{2,1,0:T(8,128)(2,1)S(1)}, u32[]{:S(2)}, u32[]{:S(2)}) async-start(bf16[8,512,256]{2,1,0:T(8,128)(2,1)} %stack.3), calls=%async_computation | async-start | bytes 4194304 | tf_op jit(solution)/shard_map/all_to_all | solution.py:49
  50.2 18.4 %copy-start.3 = (s32[64,1]{0,1:T(1,128)S(1)}, s32[64,1]{0,1:T(1,128)}, u32[]{:S(2)}) copy-start(s32[64,1]{0,1:T(1,128)} %param.14) | copy-start | bytes 772
  50.2 18.5 %copy-start = (s32[1,512]{1,0:T(1,128)S(1)}, s32[1,512]{1,0:T(1,128)}, u32[]{:S(2)}) copy-start(s32[1,512]{1,0:T(1,128)} %param.12) | copy-start | bytes 6148
  50.2 18.5 %copy-start.1 = (s32[1,64]{1,0:T(1,128)S(1)}, s32[1,64]{1,0:T(1,128)}, u32[]{:S(2)}) copy-start(s32[1,64]{1,0:T(1,128)} %param.13) | copy-start | bytes 772
  64.0 53.7 %all-to-all-start.1 = ((bf16[256,8,1024]{2,0,1:T(8,128)(2,1)}), bf16[256,8,1024]{2,0,1:T(8,128)(2,1)}, u32[]{:S(2)}, u32[]{:S(2)}) async-start(bf16[256,8,1024]{2,0,1:T(8,128)(2,1)} %copy.41), calls=%async_computation.1 | async-start | bytes 8388608 | tf_op jit(solution)/shard_map/all_to_all | solution.py:46
  69.1 68.2 %copy-start.2 = (bf16[64,8192]{1,0:T(8,128)(2,1)S(1)}, bf16[64,8192]{1,0:T(8,128)(2,1)}, u32[]{:S(2)}) copy-start(bf16[64,8192]{1,0:T(8,128)(2,1)} %param.15) | copy-start | bytes 3145732
